TPU v7x, 512 devices: a whole 4x8x8 slice. The times are simulated.
512 devices in a mesh: chan: 8 (over z), sx: 8 (over x, core), sy: 8 (over y).
Axes of the slice: x: 4, y: 8, z: 8, core: 2. Of those that a mesh axis runs over, the one named last changes fastest.
Arguments:
- volume: bfloat16 [8, 64, 64, 256], P('sx', 'sy', None, 'chan'), may hold values from -6 to 6
- kernel: bfloat16 [27, 256, 256], P(None, 'chan'), may hold values from -0.078125 to 0.078125
- grad_out: bfloat16 [8, 64, 64, 256], P('sx', 'sy', None, 'chan'), may hold values from -6 to 6
Outputs:
- out: bfloat16 [8, 64, 64, 256], P('sx', 'sy', None, 'chan')
- grad_input: bfloat16 [8, 64, 64, 256], P('sx', 'sy', None, 'chan')
- grad_kernel: float32 [27, 256, 256], P(None, 'chan')
All inputs are finite; a program needn't handle non-finite values.
Results may differ from a plain program's by a relative error of at most 0.0015.
Values may be sent and summed in bfloat16 or wider, within the bound.
No kernel may reach another device: no remote copies, remote signals or barrier semaphores. Data moves between devices by JAX's collectives and lax.ppermute only.
A program may use at most 64 MiB of HBM per device.

v0:
```python
import math
import jax
import jax.numpy as jnp
from jax import lax
from jax.sharding import PartitionSpec as P


def padded_2(shard, sides, width):
    for axis, dim in sides:
        count, length = (lax.axis_size(axis), shard.shape[dim])
        up = [(i, (i + 1) % count) for i in range(count - 1)]
        down = [(j, i) for i, j in up]
        last = lax.slice_in_dim(shard, length - width, length, axis=dim)
        leading = lax.slice_in_dim(shard, 0, width, axis=dim)
        before = lax.ppermute(last, axis, up)
        after = lax.ppermute(leading, axis, down)
        shard = jnp.concatenate([before, shard, after], axis=dim)
    return shard


def body(volume, kernel, grad_out):
    size_x, size_y, size_z, own_in = volume.shape
    total_out = kernel.shape[2]
    cells = size_x * size_y * size_z
    rim = padded_2(volume, (("sx", 0), ("sy", 1)), 1)
    padded = jnp.pad(rim, ((0, 0), (0, 0), (1, 1), (0, 0)))
    offsets = [(index // 9, index // 3 % 3, index % 3) for index in range(27)]
    partial_out = jnp.zeros((cells, total_out), jnp.float32)
    for index in range(27):
        a, b, e = offsets[index]
        window = padded[a : a + size_x, b : b + size_y, e : e + size_z].reshape(cells, own_in)
        partial_out = partial_out + jnp.dot(
            window, kernel[index], preferred_element_type=jnp.float32
        )
    partial_out = partial_out.reshape(size_x, size_y, size_z, total_out)
    out = lax.psum_scatter(partial_out, "chan", scatter_dimension=3, tiled=True).astype(
        jnp.bfloat16
    )
    grad_full = lax.all_gather(grad_out, "chan", axis=3, tiled=True)
    grad_rimmed = padded_2(grad_full, (("sx", 0), ("sy", 1)), 1)
    grad_padded = jnp.pad(grad_rimmed, ((0, 0), (0, 0), (1, 1), (0, 0)))
    flat_grad = grad_full.reshape(cells, total_out)
    back = jnp.zeros((cells, own_in), jnp.float32)
    kernel_terms = []
    for index in range(27):
        a, b, e = offsets[index]
        window = grad_padded[
            2 - a : 2 - a + size_x, 2 - b : 2 - b + size_y, 2 - e : 2 - e + size_z
        ].reshape(cells, total_out)
        back = back + lax.dot_general(
            window, kernel[index], (((1,), (1,)), ((), ())), preferred_element_type=jnp.float32
        )
        in_window = padded[a : a + size_x, b : b + size_y, e : e + size_z].reshape(cells, own_in)
        kernel_terms.append(
            lax.dot_general(
                in_window, flat_grad, (((0,), (0,)), ((), ())), preferred_element_type=jnp.float32
            )
        )
    grad_input = back.reshape(size_x, size_y, size_z, own_in).astype(jnp.bfloat16)
    local_kernel = jnp.stack(kernel_terms)
    summed = lax.psum(local_kernel, ("sx", "sy"))
    all_cells = cells * lax.axis_size("sx") * lax.axis_size("sy")
    grad_kernel = summed / jnp.float32(math.sqrt(all_cells))
    return (out, grad_input, grad_kernel)


def solution(mesh):
    return jax.shard_map(
        body,
        mesh=mesh,
        in_specs=(P("sx", "sy", None, "chan"), P(None, "chan", None), P("sx", "sy", None, "chan")),
        out_specs=(P("sx", "sy", None, "chan"), P("sx", "sy", None, "chan"), P(None, "chan", None)),
        check_vma=False,
    )
```

profile of v0, /device:TPU:25, one launch (start us, length us, event | category | flops | bytes accessed | tf_op | source)
XLA Modules:
  0.0 342.9 jit_solution(3898932481704692713)
XLA Ops:
  8.1 3.7 %collective-permute-start = (bf16[1,8,64,32]{2,3,1,0:T(8,128)(2,1)}, bf16[1,8,64,32]{2,3,1,0:T(8,128)(2,1)S(1)}, u32[]{:S(2)}, u32[]{:S(2)}) collective-permute-start(bf16[1,8,64,32]{2,3,1,0:T(8,128)(2,1)} %param.3), channel_id=1, source_target_pairs={{0,8},{8,16},{16,24},{24,32},{32,40},{40,48},{48,56},{1,9},{9,17},... | collective-permute-start | bytes 98312 | tf_op jit(solution)/shard_map/ppermute | solution.py:15
  11.7 1.9 collective-permute-start.1
  15.5 2.1 collective-permute-done.1
  17.6 2.1 collective-permute-start.3
  19.7 4.4 %collective-permute-start.2 = (bf16[3,1,64,32]{2,3,1,0:T(8,128)(2,1)S(1)}, bf16[3,1,64,32]{2,3,1,0:T(8,128)(2,1)S(1)}, u32[]{:S(2)}, u32[]{:S(2)}) collective-permute-start(bf16[3,1,64,32]{2,3,1,0:T(8,128)(2,1)S(1)} %get-tuple-element.68), channel_id=1, source_target_pairs={{0,1},{1,2},{2,3},{3,4},{4,5},{5,6},{6,7},{8,9},{9,10},{10,11},{11... | collective-permute-start | bytes 36872 | tf_op jit(solution)/shard_map/ppermute | solution.py:15
  24.1 26.2 %all_gather.3 = bf16[1,8,64,256]{2,1,0,3:T(8,128)(2,1)S(1)} all-gather(bf16[1,8,64,32]{2,1,0,3:T(8,128)(2,1)S(1)} %copy.98), channel_id=1, replica_groups=mesh['chan'=8,'sx'=8,'sy'=8] {'chan'}, dimensions={3}, use_global_device_ids=true | all-gather | bytes 294912 | tf_op jit(solution)/shard_map/all_gather | solution.py:39
  50.6 5.5 %collective-permute-start.5 = (bf16[1,8,64,256]{3,2,1,0:T(8,128)(2,1)S(1)}, bf16[1,8,64,256]{3,2,1,0:T(8,128)(2,1)S(1)}, u32[]{:S(2)}, u32[]{:S(2)}) collective-permute-start(bf16[1,8,64,256]{3,2,1,0:T(8,128)(2,1)S(1)} %copy.99), channel_id=1, source_target_pairs={{8,0},{16,8},{24,16},{32,24},{40,32},{48,40},{56,48},{9,1},{17,9},... | collective-permute-start | bytes 786440 | tf_op jit(solution)/shard_map/ppermute | solution.py:16
  56.1 4.7 %collective-permute-start.4 = (bf16[1,8,64,256]{3,2,1,0:T(8,128)(2,1)S(1)}, bf16[1,8,64,256]{3,2,1,0:T(8,128)(2,1)S(1)}, u32[]{:S(2)}, u32[]{:S(2)}) collective-permute-start(bf16[1,8,64,256]{3,2,1,0:T(8,128)(2,1)S(1)} %copy.99), channel_id=1, source_target_pairs={{0,8},{8,16},{16,24},{24,32},{32,40},{40,48},{48,56},{1,9},{9,17},... | collective-permute-start | bytes 786440 | tf_op jit(solution)/shard_map/ppermute | solution.py:15
  63.9 1.1 fusion.241
  67.0 1.4 pad_maximum_fusion.13
  73.0 1.5 copy.76
  74.5 1.6 reshape.329
  76.1 1.5 copy.77
  77.6 1.6 reshape.330
  79.2 1.5 copy.78
  80.6 1.6 reshape.331
  82.2 1.5 copy.79
  83.7 1.6 reshape.332
  85.9 1.6 reshape.333
  88.1 1.6 reshape.334
  90.3 1.6 reshape.335
  91.9 1.5 copy.84
  93.4 1.6 reshape.337
  95.0 1.5 copy.85
  96.4 1.6 reshape.338
  98.7 1.6 reshape.339
  100.9 1.6 reshape.340
  102.4 1.5 copy.88
  103.9 1.6 reshape.341
  106.1 1.6 reshape.342
  107.7 1.5 copy.90
  109.2 1.6 reshape.343
  110.7 1.5 copy.91
  112.2 1.6 reshape.344
  114.5 1.6 reshape.347
  116.8 0.9 fusion.35
  119.3 0.9 fusion.32
  121.9 0.9 fusion.29
  124.4 0.9 fusion.26
  126.9 0.9 fusion.23
  129.4 0.9 fusion.20
  146.8 1.9 collective-permute-start.7
  148.7 4.8 %collective-permute-start.6 = (bf16[3,1,64,256]{3,2,1,0:T(8,128)(2,1)S(1)}, bf16[3,1,64,256]{3,2,1,0:T(8,128)(2,1)S(1)}, u32[]{:S(2)}, u32[]{:S(2)}) collective-permute-start(bf16[3,1,64,256]{3,2,1,0:T(8,128)(2,1)S(1)} %get-tuple-element.39), channel_id=1, source_target_pairs={{0,1},{1,2},{2,3},{3,4},{4,5},{5,6},{6,7},{8,9},{9,10},{10,11},{11... | collective-permute-start | bytes 294920 | tf_op jit(solution)/shard_map/ppermute | solution.py:15
  153.8 1.3 copy.97
  155.8 0.9 fusion.240
  162.8 168.9 %all-reduce.4.cloned.1.call-done = f32[27,32,256]{2,1,0:T(8,128)} async-done(((f32[27,32,256]{2,1,0:T(8,128)}), f32[27,32,256]{2,1,0:T(8,128)}) %all-reduce.4.cloned.1.call-update) | async-done | bytes 884752 | tf_op jit(solution)/shard_map/psum | solution.py:61
  331.7 2.2 broadcast_multiply_fusion
  333.9 1.5 convert_element_type.21
  (205 shorter events, 48.3 us)
Async XLA Ops:
  8.0 52.8 %copy-start.4 = (bf16[1,8,64,32]{2,3,1,0:T(8,128)(2,1)S(1)}, bf16[1,8,64,32]{2,3,1,0:T(8,128)(2,1)}, u32[]{:S(2)}) copy-start(bf16[1,8,64,32]{2,3,1,0:T(8,128)(2,1)} %param.3) | copy-start | bytes 98308
  8.0 323.7 %all-reduce.4.cloned.1.call-start = ((), (), s32[]{:S(2)}) async-start(), calls=%async_computation.2 | async-start | bytes 1769472 | tf_op jit(solution)/shard_map/psum | solution.py:61
  8.1 6.5 %collective-permute-start = (bf16[1,8,64,32]{2,3,1,0:T(8,128)(2,1)}, bf16[1,8,64,32]{2,3,1,0:T(8,128)(2,1)S(1)}, u32[]{:S(2)}, u32[]{:S(2)}) collective-permute-start(bf16[1,8,64,32]{2,3,1,0:T(8,128)(2,1)} %param.3), channel_id=1, source_target_pairs={{0,8},{8,16},{16,24},{24,32},{32,40},{40,48},{48,56},{1,9},{9,17},... | collective-permute-start | bytes 98312 | tf_op jit(solution)/shard_map/ppermute | solution.py:15
  11.7 5.8 %collective-permute-start.1 = (bf16[1,8,64,32]{2,3,1,0:T(8,128)(2,1)}, bf16[1,8,64,32]{2,3,1,0:T(8,128)(2,1)S(1)}, u32[]{:S(2)}, u32[]{:S(2)}) collective-permute-start(bf16[1,8,64,32]{2,3,1,0:T(8,128)(2,1)} %param.3), channel_id=1, source_target_pairs={{8,0},{16,8},{24,16},{32,24},{40,32},{48,40},{56,48},{9,1},{17,9},... | collective-permute-start | bytes 98312 | tf_op jit(solution)/shard_map/ppermute | solution.py:16
  14.6 47.1 %copy-start.8 = (bf16[1,8,64,32]{2,3,1,0:T(8,128)(2,1)}, bf16[1,8,64,32]{2,3,1,0:T(8,128)(2,1)S(1)}, u32[]{:S(2)}) copy-start(bf16[1,8,64,32]{2,3,1,0:T(8,128)(2,1)S(1)} %collective-permute-done) | copy-start | bytes 98308
  17.5 45.0 %copy-start.6 = (bf16[1,8,64,32]{2,3,1,0:T(8,128)(2,1)}, bf16[1,8,64,32]{2,3,1,0:T(8,128)(2,1)S(1)}, u32[]{:S(2)}) copy-start(bf16[1,8,64,32]{2,3,1,0:T(8,128)(2,1)S(1)} %collective-permute-done.1) | copy-start | bytes 98308
  17.6 44.9 %collective-permute-start.3 = (bf16[3,1,64,32]{2,3,1,0:T(8,128)(2,1)S(1)}, bf16[3,1,64,32]{2,3,1,0:T(8,128)(2,1)S(1)}, u32[]{:S(2)}, u32[]{:S(2)}) collective-permute-start(bf16[3,1,64,32]{2,3,1,0:T(8,128)(2,1)S(1)} %get-tuple-element.69), channel_id=1, source_target_pairs={{1,0},{2,1},{3,2},{4,3},{5,4},{6,5},{7,6},{9,8},{10,9},{11,10},{12... | collective-permute-start | bytes 36872 | tf_op jit(solution)/shard_map/ppermute | solution.py:16
  19.7 42.9 %collective-permute-start.2 = (bf16[3,1,64,32]{2,3,1,0:T(8,128)(2,1)S(1)}, bf16[3,1,64,32]{2,3,1,0:T(8,128)(2,1)S(1)}, u32[]{:S(2)}, u32[]{:S(2)}) collective-permute-start(bf16[3,1,64,32]{2,3,1,0:T(8,128)(2,1)S(1)} %get-tuple-element.68), channel_id=1, source_target_pairs={{0,1},{1,2},{2,3},{3,4},{4,5},{5,6},{6,7},{8,9},{9,10},{10,11},{11... | collective-permute-start | bytes 36872 | tf_op jit(solution)/shard_map/ppermute | solution.py:15
  50.6 96.1 %collective-permute-start.5 = (bf16[1,8,64,256]{3,2,1,0:T(8,128)(2,1)S(1)}, bf16[1,8,64,256]{3,2,1,0:T(8,128)(2,1)S(1)}, u32[]{:S(2)}, u32[]{:S(2)}) collective-permute-start(bf16[1,8,64,256]{3,2,1,0:T(8,128)(2,1)S(1)} %copy.99), channel_id=1, source_target_pairs={{8,0},{16,8},{24,16},{32,24},{40,32},{48,40},{56,48},{9,1},{17,9},... | collective-permute-start | bytes 786440 | tf_op jit(solution)/shard_map/ppermute | solution.py:16
  56.1 90.7 %collective-permute-start.4 = (bf16[1,8,64,256]{3,2,1,0:T(8,128)(2,1)S(1)}, bf16[1,8,64,256]{3,2,1,0:T(8,128)(2,1)S(1)}, u32[]{:S(2)}, u32[]{:S(2)}) collective-permute-start(bf16[1,8,64,256]{3,2,1,0:T(8,128)(2,1)S(1)} %copy.99), channel_id=1, source_target_pairs={{0,8},{8,16},{16,24},{24,32},{32,40},{40,48},{48,56},{1,9},{9,17},... | collective-permute-start | bytes 786440 | tf_op jit(solution)/shard_map/ppermute | solution.py:15
  62.5 0.6 copy-start.36
  63.1 0.6 copy-start.37
  63.9 2.3 copy-start
  68.5 0.6 copy-start.2
  68.5 18.9 %copy-start.14 = (bf16[1,8,64,32]{2,3,1,0:T(8,128)(2,1)S(1)}, bf16[1,8,64,32]{2,3,1,0:T(8,128)(2,1)}, u32[]{:S(2)}) copy-start(bf16[1,8,64,32]{2,3,1,0:T(8,128)(2,1)} %get-tuple-element.51) | copy-start | bytes 98308
  68.5 21.2 %copy-start.13 = (bf16[1,8,64,32]{2,3,1,0:T(8,128)(2,1)S(1)}, bf16[1,8,64,32]{2,3,1,0:T(8,128)(2,1)}, u32[]{:S(2)}) copy-start(bf16[1,8,64,32]{2,3,1,0:T(8,128)(2,1)} %get-tuple-element.50) | copy-start | bytes 98308
  74.5 25.7 %copy-start.12 = (bf16[1,8,64,32]{2,3,1,0:T(8,128)(2,1)S(1)}, bf16[1,8,64,32]{2,3,1,0:T(8,128)(2,1)}, u32[]{:S(2)}) copy-start(bf16[1,8,64,32]{2,3,1,0:T(8,128)(2,1)} %get-tuple-element.47) | copy-start | bytes 98308
  88.1 25.7 %copy-start.11 = (bf16[1,8,64,32]{2,3,1,0:T(8,128)(2,1)S(1)}, bf16[1,8,64,32]{2,3,1,0:T(8,128)(2,1)}, u32[]{:S(2)}) copy-start(bf16[1,8,64,32]{2,3,1,0:T(8,128)(2,1)} %get-tuple-element.42) | copy-start | bytes 98308
  90.3 25.7 %copy-start.3 = (bf16[1,8,64,32]{2,3,1,0:T(8,128)(2,1)S(1)}, bf16[1,8,64,32]{2,3,1,0:T(8,128)(2,1)}, u32[]{:S(2)}) copy-start(bf16[1,8,64,32]{2,3,1,0:T(8,128)(2,1)} %copy-done.2) | copy-start | bytes 98308
  102.4 16.1 %copy-start.9 = (bf16[1,8,64,32]{2,3,1,0:T(8,128)(2,1)S(1)}, bf16[1,8,64,32]{2,3,1,0:T(8,128)(2,1)}, u32[]{:S(2)}) copy-start(bf16[1,8,64,32]{2,3,1,0:T(8,128)(2,1)} %copy-done.8) | copy-start | bytes 98308
  116.0 5.0 %copy-start.1 = (bf16[1,8,64,32]{2,3,1,0:T(8,128)(2,1)S(1)}, bf16[1,8,64,32]{2,3,1,0:T(8,128)(2,1)}, u32[]{:S(2)}) copy-start(bf16[1,8,64,32]{2,3,1,0:T(8,128)(2,1)} %get-tuple-element.60) | copy-start | bytes 98308
  121.0 5.0 %copy-start.5 = (bf16[1,8,64,32]{2,3,1,0:T(8,128)(2,1)S(1)}, bf16[1,8,64,32]{2,3,1,0:T(8,128)(2,1)}, u32[]{:S(2)}) copy-start(bf16[1,8,64,32]{2,3,1,0:T(8,128)(2,1)} %param.3) | copy-start | bytes 98308
  128.6 5.0 %copy-start.7 = (bf16[1,8,64,32]{2,3,1,0:T(8,128)(2,1)S(1)}, bf16[1,8,64,32]{2,3,1,0:T(8,128)(2,1)}, u32[]{:S(2)}) copy-start(bf16[1,8,64,32]{2,3,1,0:T(8,128)(2,1)} %copy-done.6) | copy-start | bytes 98308
  134.4 3.5 %copy-start.17 = (bf16[512,32]{0,1:T(8,128)(2,1)S(1)}, bf16[512,32]{0,1:T(8,128)(2,1)}, u32[]{:S(2)}) copy-start(bf16[512,32]{0,1:T(8,128)(2,1)} %reshape.324) | copy-start | bytes 98308
  136.9 1.2 copy-start.21
  137.8 0.8 copy-start.25
  137.8 196.1 %reduce-scatter.2.cloned.1.call-start = ((), (), s32[]{:S(2)}) async-start(), calls=%async_computation.1 | async-start | bytes 1179648 | tf_op jit(solution)/shard_map/reduce_scatter | solution.py:36
  138.2 0.8 copy-start.16
  138.6 0.8 copy-start.18
  138.9 0.8 copy-start.19
  139.3 0.8 copy-start.20
  139.7 0.8 copy-start.22
  140.1 0.8 copy-start.23
  140.4 0.8 copy-start.26
  140.9 0.8 copy-start.29
  141.2 0.8 copy-start.15
  141.6 0.8 copy-start.24
  142.0 0.8 copy-start.27
  142.4 0.8 copy-start.28
  142.7 0.8 copy-start.30
  143.2 0.8 copy-start.32
  143.5 0.8 copy-start.33
  143.9 0.8 copy-start.34
  144.3 0.8 copy-start.35
  145.0 0.8 copy-start.31
  145.8 0.8 copy-start.10
  146.8 8.3 %collective-permute-start.7 = (bf16[3,1,64,256]{3,2,1,0:T(8,128)(2,1)S(1)}, bf16[3,1,64,256]{3,2,1,0:T(8,128)(2,1)S(1)}, u32[]{:S(2)}, u32[]{:S(2)}) collective-permute-start(bf16[3,1,64,256]{3,2,1,0:T(8,128)(2,1)S(1)} %get-tuple-element.40), channel_id=1, source_target_pairs={{1,0},{2,1},{3,2},{4,3},{5,4},{6,5},{7,6},{9,8},{10,9},{11,10},{12... | collective-permute-start | bytes 294920 | tf_op jit(solution)/shard_map/ppermute | solution.py:16
  148.7 6.4 %collective-permute-start.6 = (bf16[3,1,64,256]{3,2,1,0:T(8,128)(2,1)S(1)}, bf16[3,1,64,256]{3,2,1,0:T(8,128)(2,1)S(1)}, u32[]{:S(2)}, u32[]{:S(2)}) collective-permute-start(bf16[3,1,64,256]{3,2,1,0:T(8,128)(2,1)S(1)} %get-tuple-element.39), channel_id=1, source_target_pairs={{0,1},{1,2},{2,3},{3,4},{4,5},{5,6},{6,7},{8,9},{9,10},{10,11},{11... | collective-permute-start | bytes 294920 | tf_op jit(solution)/shard_map/ppermute | solution.py:15
Sparse Core Ops, SparseCore 0:
  137.9 193.7 all-reduce.3
Sparse Core Ops, SparseCore 1:
  155.2 32.7 reduce-scatter.1
where the time goes:
time: 345 us; the launch traced here: 343 us
  waiting for transfers between devices  171 us (50%)
  local copies, waits for them, and re-layouts  60 us (17%)
  matrix products  34.2 us (10%)
  starting transfers between devices  29 us (8%)
  blocking collectives  26.2 us (8%)
  between operations  16.2 us (5%)
  other arithmetic  6.23 us (2%)
    psum x1, waiting for transfers between devices, body(): summed = lax.psum(local_kernel, ('sx', 'sy'))  169 us
    reshape x27, local copies, waits for them, and re-layouts, body(): padded[a:a + size_x, b:b + size_y, e:e + size_z].reshape(cells, own_in)  29.3 us
    all_gather x1, blocking collectives, body(): grad_full = lax.all_gather(grad_out, 'chan', axis=3, tiled=True)  26.2 us
    dot_general x27, matrix products, body(): lax.dot_general(in_window, flat_grad, (((0,), (0,)), ((), ())), preferred...  22.6 us
    slice x25, local copies, waits for them, and re-layouts, body(): padded[a:a + size_x, b:b + size_y, e:e + size_z].reshape(cells, own_in)  21 us
    ppermute x4, starting transfers between devices, padded_2(): before = lax.ppermute(last, axis, up)  17.6 us
    ppermute x4, starting transfers between devices, padded_2(): after = lax.ppermute(leading, axis, down)  11.4 us
    unnamed x81, local copies, waits for them, and re-layouts  6.98 us
  transfers between devices with their start and end apart: 10, of which 2 were waited for; matrix products, arithmetic and copies ran while one was open for 28% of the time, Pallas kernels for 0%

commit v1 on v0

--- a/solution.py
+++ b/solution.py
@@ -36,7 +36,23 @@
     out = lax.psum_scatter(partial_out, "chan", scatter_dimension=3, tiled=True).astype(
         jnp.bfloat16
     )
-    grad_full = lax.all_gather(grad_out, "chan", axis=3, tiled=True)
+    ways, here, step = (lax.axis_size("chan"), lax.axis_index("chan"), grad_out.shape[3])
+    dims = [n * ways if d == 3 else n for d, n in enumerate(grad_out.shape)]
+    full = lax.dynamic_update_slice_in_dim(
+        jnp.zeros(dims, grad_out.dtype), grad_out, here * step, axis=3
+    )
+    going_up = going_down = grad_out
+    for far in range(1, ways // 2 + 1):
+        going_up = lax.ppermute(going_up, "chan", [(d, (d + 1) % ways) for d in range(ways)])
+        full = lax.dynamic_update_slice_in_dim(full, going_up, (here - far) % ways * step, axis=3)
+        if 2 * far < ways:
+            going_down = lax.ppermute(
+                going_down, "chan", [(d, (d - 1) % ways) for d in range(ways)]
+            )
+            full = lax.dynamic_update_slice_in_dim(
+                full, going_down, (here + far) % ways * step, axis=3
+            )
+    grad_full = full
     grad_rimmed = padded_2(grad_full, (("sx", 0), ("sy", 1)), 1)
     grad_padded = jnp.pad(grad_rimmed, ((0, 0), (0, 0), (1, 1), (0, 0)))
     flat_grad = grad_full.reshape(cells, total_out)

time: 345 us -> 308 us (0.89)
  local copies, waits for them, and re-layouts: 60 us -> 33.3 us
  blocking collectives: 26.2 us -> 0 us
  starting transfers between devices: 29 us -> 53.5 us
  matrix products: 34.2 us -> 17.5 us
  waiting for transfers between devices: 171 us -> 179 us
    ppermute x0 -> x7, starting transfers between devices: none -> 27.7 us  [the longest x3 17.7 us: body(): lax.ppermute(going_down, 'chan', [(d, (d - 1) % ways) for d in range(ways)])]
    all_gather x1 -> x0, blocking collectives: 26.2 us -> none  [body(): grad_full = lax.all_gather(grad_out, 'chan', axis=3, tiled=True)]
    reshape x27, local copies, waits for them, and re-layouts: 29.3 us -> 6.79 us  [body(): padded[a:a + size_x, b:b + size_y, e:e + size_z].reshape(cells, own_in)]
    slice x25, local copies, waits for them, and re-layouts: 21 us -> 2.45 us  [body(): padded[a:a + size_x, b:b + size_y, e:e + size_z].reshape(cells, own_in)]
    dot_general x27, matrix products: 22.6 us -> 5.84 us  [body(): lax.dot_general(in_window, flat_grad, (((0,), (0,)), ((), ())), preferred...]
    dynamic_update_slice x0 -> x8, local copies, waits for them, and re-layouts: none -> 11.8 us  [the longest x4 5.72 us: body(): lax.dynamic_update_slice_in_dim(full, going_up, (here - far) % ways * ste...]
    psum x1, waiting for transfers between devices: 169 us -> 179 us  [body(): summed = lax.psum(local_kernel, ('sx', 'sy'))]
    ppermute x0 -> x7, local copies, waits for them, and re-layouts: none -> 4.2 us  [the longest x4 2.16 us: body(): lax.ppermute(going_up, 'chan', [(d, (d + 1) % ways) for d in range(ways)])]
  transfers between devices with their start and end apart: 10 -> 17, of which waited for: 2 -> 2; matrix products, arithmetic and copies ran while one was open for 28% -> 17% of each run, Pallas kernels for 0% -> 0%
where the time goes in v1:
time: 308 us; the launch traced here: 307 us
  waiting for transfers between devices  179 us (58%)
  starting transfers between devices  53.5 us (17%)
  local copies, waits for them, and re-layouts  33.3 us (11%)
  matrix products  17.5 us (6%)
  between operations  16.8 us (5%)
  other arithmetic  6.35 us (2%)
    psum x1, waiting for transfers between devices, body(): summed = lax.psum(local_kernel, ('sx', 'sy'))  179 us
    ppermute x3, starting transfers between devices, body(): lax.ppermute(going_down, 'chan', [(d, (d - 1) % ways) for d in range(ways)])  17.7 us
    ppermute x4, starting transfers between devices, padded_2(): before = lax.ppermute(last, axis, up)  17.5 us
    ppermute x4, starting transfers between devices, body(): lax.ppermute(going_up, 'chan', [(d, (d + 1) % ways) for d in range(ways)])  9.93 us
    ppermute x4, starting transfers between devices, padded_2(): after = lax.ppermute(leading, axis, down)  8.23 us
    reshape x27, local copies, waits for them, and re-layouts, body(): padded[a:a + size_x, b:b + size_y, e:e + size_z].reshape(cells, own_in)  6.79 us
    dot_general x27, matrix products, body(): jnp.dot(window, kernel[index], preferred_element_type=jnp.float32)  6.63 us
  transfers between devices with their start and end apart: 17, of which 2 were waited for; matrix products, arithmetic and copies ran while one was open for 17% of the time, Pallas kernels for 0%

profile of v1, /device:TPU:25, one launch (start us, length us, event | category | flops | bytes accessed | tf_op | source)
XLA Modules:
  0.0 306.9 jit_solution(12535437286542561735)
XLA Ops:
  8.0 3.7 %collective-permute-start = (bf16[1,8,64,32]{2,3,1,0:T(8,128)(2,1)}, bf16[1,8,64,32]{2,3,1,0:T(8,128)(2,1)S(1)}, u32[]{:S(2)}, u32[]{:S(2)}) collective-permute-start(bf16[1,8,64,32]{2,3,1,0:T(8,128)(2,1)} %param.3), channel_id=1, source_target_pairs={{0,8},{8,16},{16,24},{24,32},{32,40},{40,48},{48,56},{1,9},{9,17},... | collective-permute-start | bytes 98312 | tf_op jit(solution)/shard_map/ppermute | solution.py:15
  11.7 1.9 collective-permute-start.1
  13.7 4.0 %collective-permute-start.4 = (bf16[1,8,64,32]{2,3,1,0:T(8,128)(2,1)}, bf16[1,8,64,32]{2,3,1,0:T(8,128)(2,1)}, u32[]{:S(2)}, u32[]{:S(2)}) collective-permute-start(bf16[1,8,64,32]{2,3,1,0:T(8,128)(2,1)} %param.5), channel_id=1, source_target_pairs={{0,64},{64,128},{128,192},{192,256},{256,320},{320,384},{384,448},... | collective-permute-start | bytes 98312 | tf_op jit(solution)/shard_map/ppermute | solution.py:46
  17.7 8.6 %collective-permute-start.5 = (bf16[1,8,64,32]{2,3,1,0:T(8,128)(2,1)}, bf16[1,8,64,32]{2,3,1,0:T(8,128)(2,1)}, u32[]{:S(2)}, u32[]{:S(2)}) collective-permute-start(bf16[1,8,64,32]{2,3,1,0:T(8,128)(2,1)} %param.5), channel_id=1, source_target_pairs={{0,448},{64,0},{128,64},{192,128},{256,192},{320,256},{384,320},{4... | collective-permute-start | bytes 98312 | tf_op jit(solution)/shard_map/ppermute | solution.py:49
  26.3 0.9 constant_dynamic-update-slice_fusion.1
  27.2 2.1 collective-permute-start.3
  29.3 4.4 %collective-permute-start.2 = (bf16[3,1,64,32]{2,3,1,0:T(8,128)(2,1)S(1)}, bf16[3,1,64,32]{2,3,1,0:T(8,128)(2,1)S(1)}, u32[]{:S(2)}, u32[]{:S(2)}) collective-permute-start(bf16[3,1,64,32]{2,3,1,0:T(8,128)(2,1)S(1)} %get-tuple-element.62), channel_id=1, source_target_pairs={{0,1},{1,2},{2,3},{3,4},{4,5},{5,6},{6,7},{8,9},{9,10},{10,11},{11... | collective-permute-start | bytes 36872 | tf_op jit(solution)/shard_map/ppermute | solution.py:15
  33.7 0.9 copy.29
  34.6 1.0 copy.44
  35.7 0.7 reshape.336
  36.4 0.5 dynamic_update_slice.24
  37.0 0.7 reshape.327
  37.8 0.7 reshape.345
  38.5 1.0 copy.45
  39.5 1.8 dynamic_update_slice.25
  41.2 1.0 copy.46
  42.2 1.8 dynamic_update_slice.26
  44.0 1.9 collective-permute-start.6
  46.0 4.6 %collective-permute-start.7 = (bf16[1,8,64,32]{2,3,1,0:T(8,128)(2,1)}, bf16[1,8,64,32]{2,3,1,0:T(8,128)(2,1)}, u32[]{:S(2)}, u32[]{:S(2)}) collective-permute-start(bf16[1,8,64,32]{2,3,1,0:T(8,128)(2,1)} %collective-permute-done.5), channel_id=1, source_target_pairs={{0,448},{64,0},{128,64},{192,128},{256,192},{320,256},{384,320},{4... | collective-permute-start | bytes 98312 | tf_op jit(solution)/shard_map/ppermute | solution.py:49
  50.6 0.6 copy-done.12
  51.2 0.9 fusion.76
  52.1 0.9 fusion.243
  53.0 0.7 reshape.346
  54.6 0.8 pad_maximum_fusion.13
  55.6 0.9 copy.18
  56.6 0.7 reshape.326
  65.7 1.9 collective-permute-start.8
  68.1 4.6 %collective-permute-start.9 = (bf16[1,8,64,32]{2,3,1,0:T(8,128)(2,1)}, bf16[1,8,64,32]{2,3,1,0:T(8,128)(2,1)S(1)}, u32[]{:S(2)}, u32[]{:S(2)}) collective-permute-start(bf16[1,8,64,32]{2,3,1,0:T(8,128)(2,1)} %collective-permute-done.7), channel_id=1, source_target_pairs={{0,448},{64,0},{128,64},{192,128},{256,192},{320,256},{384,320},{4... | collective-permute-start | bytes 98312 | tf_op jit(solution)/shard_map/ppermute | solution.py:49
  73.1 2.1 collective-permute-start.10
  75.5 0.7 reshape.348
  76.2 1.0 copy.47
  77.2 1.8 dynamic_update_slice.27
  78.9 1.0 copy.48
  79.9 1.8 dynamic_update_slice.28
  81.9 1.8 dynamic_update_slice.29
  83.8 1.8 dynamic_update_slice.30
  86.2 2.3 collective-permute-start.12
  88.5 4.9 %collective-permute-start.11 = (bf16[1,8,64,256]{3,2,1,0:T(8,128)(2,1)S(1)}, bf16[1,8,64,256]{3,2,1,0:T(8,128)(2,1)S(1)}, u32[]{:S(2)}, u32[]{:S(2)}) collective-permute-start(bf16[1,8,64,256]{3,2,1,0:T(8,128)(2,1)S(1)} %dynamic_update_slice.31), channel_id=1, source_target_pairs={{0,8},{8,16},{16,24},{24,32},{32,40},{40,48},{48,56},{1,9},{9,17},... | collective-permute-start | bytes 786440 | tf_op jit(solution)/shard_map/ppermute | solution.py:15
  99.5 0.9 copy-done.1
  101.0 1.9 collective-permute-start.14
  102.9 4.6 %collective-permute-start.13 = (bf16[3,1,64,256]{3,2,1,0:T(8,128)(2,1)S(1)}, bf16[3,1,64,256]{3,2,1,0:T(8,128)(2,1)S(1)}, u32[]{:S(2)}, u32[]{:S(2)}) collective-permute-start(bf16[3,1,64,256]{3,2,1,0:T(8,128)(2,1)S(1)} %get-tuple-element.33), channel_id=1, source_target_pairs={{0,1},{1,2},{2,3},{3,4},{4,5},{5,6},{6,7},{8,9},{9,10},{10,11},{11... | collective-permute-start | bytes 294920 | tf_op jit(solution)/shard_map/ppermute | solution.py:15
  107.7 1.3 copy.43
  109.1 0.6 select_maximum_fusion
  109.7 0.9 fusion.242
  116.1 0.6 copy.52
  116.8 178.9 %all-reduce.4.cloned.1.call-done = f32[27,32,256]{2,1,0:T(8,128)} async-done(((f32[27,32,256]{2,1,0:T(8,128)}), f32[27,32,256]{2,1,0:T(8,128)}) %all-reduce.4.cloned.1.call-update) | async-done | bytes 884752 | tf_op jit(solution)/shard_map/psum | solution.py:77
  295.7 2.2 broadcast_multiply_fusion
  297.9 1.5 convert_element_type.21
  (183 shorter events, 23.3 us)
Async XLA Ops:
  8.0 287.7 %all-reduce.4.cloned.1.call-start = ((), (), s32[]{:S(2)}) async-start(), calls=%async_computation.2 | async-start | bytes 1769472 | tf_op jit(solution)/shard_map/psum | solution.py:77
  8.0 18.2 %collective-permute-start = (bf16[1,8,64,32]{2,3,1,0:T(8,128)(2,1)}, bf16[1,8,64,32]{2,3,1,0:T(8,128)(2,1)S(1)}, u32[]{:S(2)}, u32[]{:S(2)}) collective-permute-start(bf16[1,8,64,32]{2,3,1,0:T(8,128)(2,1)} %param.3), channel_id=1, source_target_pairs={{0,8},{8,16},{16,24},{24,32},{32,40},{40,48},{48,56},{1,9},{9,17},... | collective-permute-start | bytes 98312 | tf_op jit(solution)/shard_map/ppermute | solution.py:15
  11.7 15.5 %collective-permute-start.1 = (bf16[1,8,64,32]{2,3,1,0:T(8,128)(2,1)}, bf16[1,8,64,32]{2,3,1,0:T(8,128)(2,1)S(1)}, u32[]{:S(2)}, u32[]{:S(2)}) collective-permute-start(bf16[1,8,64,32]{2,3,1,0:T(8,128)(2,1)} %param.3), channel_id=1, source_target_pairs={{8,0},{16,8},{24,16},{32,24},{40,32},{48,40},{56,48},{9,1},{17,9},... | collective-permute-start | bytes 98312 | tf_op jit(solution)/shard_map/ppermute | solution.py:16
  13.7 24.8 %collective-permute-start.4 = (bf16[1,8,64,32]{2,3,1,0:T(8,128)(2,1)}, bf16[1,8,64,32]{2,3,1,0:T(8,128)(2,1)}, u32[]{:S(2)}, u32[]{:S(2)}) collective-permute-start(bf16[1,8,64,32]{2,3,1,0:T(8,128)(2,1)} %param.5), channel_id=1, source_target_pairs={{0,64},{64,128},{128,192},{192,256},{256,320},{320,384},{384,448},... | collective-permute-start | bytes 98312 | tf_op jit(solution)/shard_map/ppermute | solution.py:46
  17.7 23.6 %collective-permute-start.5 = (bf16[1,8,64,32]{2,3,1,0:T(8,128)(2,1)}, bf16[1,8,64,32]{2,3,1,0:T(8,128)(2,1)}, u32[]{:S(2)}, u32[]{:S(2)}) collective-permute-start(bf16[1,8,64,32]{2,3,1,0:T(8,128)(2,1)} %param.5), channel_id=1, source_target_pairs={{0,448},{64,0},{128,64},{192,128},{256,192},{320,256},{384,320},{4... | collective-permute-start | bytes 98312 | tf_op jit(solution)/shard_map/ppermute | solution.py:49
  26.3 13.2 %copy-start.3 = (bf16[1,8,64,32]{2,3,1,0:T(8,128)(2,1)}, bf16[1,8,64,32]{2,3,1,0:T(8,128)(2,1)S(1)}, u32[]{:S(2)}) copy-start(bf16[1,8,64,32]{2,3,1,0:T(8,128)(2,1)S(1)} %collective-permute-done) | copy-start | bytes 98308
  27.2 23.3 %collective-permute-start.3 = (bf16[3,1,64,32]{2,3,1,0:T(8,128)(2,1)S(1)}, bf16[3,1,64,32]{2,3,1,0:T(8,128)(2,1)}, u32[]{:S(2)}, u32[]{:S(2)}) collective-permute-start(bf16[3,1,64,32]{2,3,1,0:T(8,128)(2,1)S(1)} %get-tuple-element.63), channel_id=1, source_target_pairs={{1,0},{2,1},{3,2},{4,3},{5,4},{6,5},{7,6},{9,8},{10,9},{11,10},{12... | collective-permute-start | bytes 36872 | tf_op jit(solution)/shard_map/ppermute | solution.py:16
  29.3 21.3 %collective-permute-start.2 = (bf16[3,1,64,32]{2,3,1,0:T(8,128)(2,1)S(1)}, bf16[3,1,64,32]{2,3,1,0:T(8,128)(2,1)S(1)}, u32[]{:S(2)}, u32[]{:S(2)}) collective-permute-start(bf16[3,1,64,32]{2,3,1,0:T(8,128)(2,1)S(1)} %get-tuple-element.62), channel_id=1, source_target_pairs={{0,1},{1,2},{2,3},{3,4},{4,5},{5,6},{6,7},{8,9},{9,10},{10,11},{11... | collective-permute-start | bytes 36872 | tf_op jit(solution)/shard_map/ppermute | solution.py:15
  44.0 21.6 %collective-permute-start.6 = (bf16[1,8,64,32]{2,3,1,0:T(8,128)(2,1)}, bf16[1,8,64,32]{2,3,1,0:T(8,128)(2,1)}, u32[]{:S(2)}, u32[]{:S(2)}) collective-permute-start(bf16[1,8,64,32]{2,3,1,0:T(8,128)(2,1)} %collective-permute-done.4), channel_id=1, source_target_pairs={{0,64},{64,128},{128,192},{192,256},{256,320},{320,384},{384,448},... | collective-permute-start | bytes 98312 | tf_op jit(solution)/shard_map/ppermute | solution.py:46
  46.0 22.1 %collective-permute-start.7 = (bf16[1,8,64,32]{2,3,1,0:T(8,128)(2,1)}, bf16[1,8,64,32]{2,3,1,0:T(8,128)(2,1)}, u32[]{:S(2)}, u32[]{:S(2)}) collective-permute-start(bf16[1,8,64,32]{2,3,1,0:T(8,128)(2,1)} %collective-permute-done.5), channel_id=1, source_target_pairs={{0,448},{64,0},{128,64},{192,128},{256,192},{320,256},{384,320},{4... | collective-permute-start | bytes 98312 | tf_op jit(solution)/shard_map/ppermute | solution.py:49
  50.6 0.6 copy-start.12
  52.1 2.0 copy-start
  59.6 0.8 copy-start.11
  59.9 0.8 copy-start.8
  62.2 0.8 copy-start.6
  64.7 0.8 copy-start.9
  64.9 2.7 copy-start.7
  65.7 7.4 %collective-permute-start.8 = (bf16[1,8,64,32]{2,3,1,0:T(8,128)(2,1)}, bf16[1,8,64,32]{2,3,1,0:T(8,128)(2,1)S(1)}, u32[]{:S(2)}, u32[]{:S(2)}) collective-permute-start(bf16[1,8,64,32]{2,3,1,0:T(8,128)(2,1)} %collective-permute-done.6), channel_id=1, source_target_pairs={{0,64},{64,128},{128,192},{192,256},{256,320},{320,384},{384,448},... | collective-permute-start | bytes 98312 | tf_op jit(solution)/shard_map/ppermute | solution.py:46
  68.1 15.6 %collective-permute-start.9 = (bf16[1,8,64,32]{2,3,1,0:T(8,128)(2,1)}, bf16[1,8,64,32]{2,3,1,0:T(8,128)(2,1)S(1)}, u32[]{:S(2)}, u32[]{:S(2)}) collective-permute-start(bf16[1,8,64,32]{2,3,1,0:T(8,128)(2,1)} %collective-permute-done.7), channel_id=1, source_target_pairs={{0,448},{64,0},{128,64},{192,128},{256,192},{320,256},{384,320},{4... | collective-permute-start | bytes 98312 | tf_op jit(solution)/shard_map/ppermute | solution.py:49
  73.1 12.5 %collective-permute-start.10 = (bf16[1,8,64,32]{2,3,1,0:T(8,128)(2,1)S(1)}, bf16[1,8,64,32]{2,3,1,0:T(8,128)(2,1)S(1)}, u32[]{:S(2)}, u32[]{:S(2)}) collective-permute-start(bf16[1,8,64,32]{2,3,1,0:T(8,128)(2,1)S(1)} %collective-permute-done.8), channel_id=1, source_target_pairs={{0,64},{64,128},{128,192},{192,256},{256,320},{320,384},{384,448},... | collective-permute-start | bytes 98312 | tf_op jit(solution)/shard_map/ppermute | solution.py:46
  83.8 10.5 %copy-start.4 = (bf16[1,8,64,32]{2,3,1,0:T(8,128)(2,1)S(1)}, bf16[1,8,64,32]{2,3,1,0:T(8,128)(2,1)}, u32[]{:S(2)}) copy-start(bf16[1,8,64,32]{2,3,1,0:T(8,128)(2,1)} %copy-done.3) | copy-start | bytes 98308
  86.2 14.7 %collective-permute-start.12 = (bf16[1,8,64,256]{3,2,1,0:T(8,128)(2,1)S(1)}, bf16[1,8,64,256]{3,2,1,0:T(8,128)(2,1)S(1)}, u32[]{:S(2)}, u32[]{:S(2)}) collective-permute-start(bf16[1,8,64,256]{3,2,1,0:T(8,128)(2,1)S(1)} %dynamic_update_slice.31), channel_id=1, source_target_pairs={{8,0},{16,8},{24,16},{32,24},{40,32},{48,40},{56,48},{9,1},{17,9},... | collective-permute-start | bytes 786440 | tf_op jit(solution)/shard_map/ppermute | solution.py:16
  88.5 12.4 %collective-permute-start.11 = (bf16[1,8,64,256]{3,2,1,0:T(8,128)(2,1)S(1)}, bf16[1,8,64,256]{3,2,1,0:T(8,128)(2,1)S(1)}, u32[]{:S(2)}, u32[]{:S(2)}) collective-permute-start(bf16[1,8,64,256]{3,2,1,0:T(8,128)(2,1)S(1)} %dynamic_update_slice.31), channel_id=1, source_target_pairs={{0,8},{8,16},{16,24},{24,32},{32,40},{40,48},{48,56},{1,9},{9,17},... | collective-permute-start | bytes 786440 | tf_op jit(solution)/shard_map/ppermute | solution.py:15
  95.0 1.4 copy-start.2
  98.5 2.0 copy-start.10
  99.2 1.5 copy-start.5
  99.5 0.9 copy-start.1
  100.4 197.4 %reduce-scatter.2.cloned.1.call-start = ((), (), s32[]{:S(2)}) async-start(), calls=%async_computation.1 | async-start | bytes 1179648 | tf_op jit(solution)/shard_map/reduce_scatter | solution.py:36
  101.0 8.1 %collective-permute-start.14 = (bf16[3,1,64,256]{3,2,1,0:T(8,128)(2,1)S(1)}, bf16[3,1,64,256]{3,2,1,0:T(8,128)(2,1)S(1)}, u32[]{:S(2)}, u32[]{:S(2)}) collective-permute-start(bf16[3,1,64,256]{3,2,1,0:T(8,128)(2,1)S(1)} %get-tuple-element.34), channel_id=1, source_target_pairs={{1,0},{2,1},{3,2},{4,3},{5,4},{6,5},{7,6},{9,8},{10,9},{11,10},{12... | collective-permute-start | bytes 294920 | tf_op jit(solution)/shard_map/ppermute | solution.py:16
  102.9 6.2 %collective-permute-start.13 = (bf16[3,1,64,256]{3,2,1,0:T(8,128)(2,1)S(1)}, bf16[3,1,64,256]{3,2,1,0:T(8,128)(2,1)S(1)}, u32[]{:S(2)}, u32[]{:S(2)}) collective-permute-start(bf16[3,1,64,256]{3,2,1,0:T(8,128)(2,1)S(1)} %get-tuple-element.33), channel_id=1, source_target_pairs={{0,1},{1,2},{2,3},{3,4},{4,5},{5,6},{6,7},{8,9},{9,10},{10,11},{11... | collective-permute-start | bytes 294920 | tf_op jit(solution)/shard_map/ppermute | solution.py:15
Sparse Core Ops, SparseCore 0:
  100.6 195.0 all-reduce.3
Sparse Core Ops, SparseCore 1:
  109.2 33.5 reduce-scatter.1
